TPU v7x, 128 devices: a whole 4x4x4 slice. The times are simulated.
128 devices in a mesh: dp: 64 (over z, y, x), fsdp: 2 (over core).
Axes of the slice: x: 4, y: 4, z: 4, core: 2. Of those that a mesh axis runs over, the one named last changes fastest.
Arguments:
- mel_panels: bfloat16 [8192, 10240], P(('dp', 'fsdp')), may hold values from -6 to 6
- frames: int32 [8192], P(('dp', 'fsdp')), may hold values from 0 to 128, as said below
- target: int32 [8192], P(('dp', 'fsdp')), may hold values from 0 to 63, as said below
- conv_first: bfloat16 [9, 256], P(None, 'fsdp'), may hold values from -2 to 2
- depth_a: bfloat16 [9, 256], P(None, 'fsdp'), may hold values from -3 to 3
- point_a: bfloat16 [256, 256], P(None, 'fsdp'), may hold values from -0.5 to 0.5
- depth_b: bfloat16 [9, 256], P(None, 'fsdp'), may hold values from -3 to 3
- point_b: bfloat16 [256, 256], P(None, 'fsdp'), may hold values from -0.5 to 0.5
- linear_weight: bfloat16 [2560, 1024], P(None, 'fsdp'), may hold values from -0.15625 to 0.15625
- norm_gain: bfloat16 [1024], P('fsdp'), may hold values from 0.099609375 to 1.8984375
- up_weight: bfloat16 [1024, 2048], P(None, 'fsdp'), may hold values from -0.1875 to 0.1875
- depth_kernel: bfloat16 [9, 1024], P(None, 'fsdp'), may hold values from -2 to 2
- conv_gain: bfloat16 [1024], P('fsdp'), may hold values from 0.099609375 to 1.8984375
- down_weight: bfloat16 [1024, 1024], P('fsdp'), may hold values from -0.1875 to 0.1875
- cotangent: bfloat16 [65536, 1024], P(('dp', 'fsdp')), may hold values from -6 to 6
Outputs:
- layer_out: bfloat16 [65536, 1024], P(('dp', 'fsdp'))
- grad_input: bfloat16 [65536, 1024], P(('dp', 'fsdp'))
- grad_down: float32 [1024, 1024], P('fsdp')
Inputs may be any that keep to these rules, and one draw needn't show every extreme that they name: The slots of one loader are those of one index of dp and fsdp. A live slot holds a panel of 8 * m frames with 8 * m >= 32; frames = 0 marks an empty slot. Every device receives exactly 32 panels from the loaders of its own fsdp index, at most one from any loader, and one of them has 128 frames. `target`: only live slots are sent.
All inputs are finite; a program needn't handle non-finite values.
Results may differ from a plain program's by a relative error of at most 0.017.
Values may be sent and summed in bfloat16 or wider, within the bound.
A program may use at most 192 MiB of HBM per device.

v0:
```python
import math
import jax
import jax.numpy as jnp
from jax import lax
from jax.sharding import PartitionSpec as P

MELS = 80
PANEL = 128
EPSILON = 1e-05


def sent_together(arrays, axis, dim, along):
    widths = [a.shape[along] for a in arrays]
    both = jnp.concatenate(arrays, axis=along)
    out = lax.all_gather(both, axis, axis=dim, tiled=True)
    return tuple(jnp.split(out, [sum(widths[:k]) for k in range(1, len(widths))], axis=along))


def in_order(tiles, dim):
    dims = list(tiles.shape[1:])
    dims[dim] *= tiles.shape[0]
    return jnp.moveaxis(tiles, 0, dim).reshape(dims)


def gather_together(arrays, axis, dims):
    line = jnp.concatenate([a.reshape(-1) for a in arrays])
    lines, at, done = (lax.all_gather(line, axis), 0, [])
    for a, dim in zip(arrays, dims):
        tiles = lines[:, at : at + a.size].reshape(-1, *a.shape)
        done.append(in_order(tiles, dim))
        at += a.size
    return tuple(done)


def in_blocks(value, dim, size):
    before, after = (value.shape[:dim], value.shape[dim + 1 :])
    return jnp.moveaxis(value.reshape(*before, size, -1, *after), dim, 0)


def sent_and_summed(value, axis, dim):
    size = lax.axis_size(axis)
    tiles = lax.all_to_all(in_blocks(value, dim, size), axis, 0, 0, tiled=True)
    return jnp.sum(tiles.astype(jnp.float32), axis=0)


def phase_rows(source):
    shape_in = source.shape
    split = source.reshape((shape_in[0], shape_in[1] // 2, 2) + shape_in[2:])
    even = split[:, :, 0]
    odd = split[:, :, 1]
    before = jnp.concatenate([jnp.zeros_like(odd[:, :1]), odd[:, :-1]], axis=1)
    return (before, even, odd)


def phase_cols(source):
    shape_in = source.shape
    split = source.reshape(shape_in[:2] + (shape_in[2] // 2, 2) + shape_in[3:])
    even = split[:, :, :, 0]
    odd = split[:, :, :, 1]
    before = jnp.concatenate([jnp.zeros_like(odd[:, :, :1]), odd[:, :, :-1]], axis=2)
    return (before, even, odd)


def first_section(masked, weights):
    height = masked.shape[1] // 2
    breadth = masked.shape[2] // 2
    summed = jnp.zeros((masked.shape[0], height, breadth, weights.shape[1]), jnp.float32)
    row_views = phase_rows(masked)
    for i in range(3):
        col_views = phase_cols(row_views[i])
        for j in range(3):
            window = col_views[j].astype(jnp.float32)
            summed = summed + window[:, :, :, None] * weights[3 * i + j].astype(jnp.float32)
    return jnp.maximum(summed, 0.0).astype(jnp.bfloat16)


def depth_stride(source, weights):
    height = source.shape[1] // 2
    breadth = source.shape[2] // 2
    summed = jnp.zeros((source.shape[0], height, breadth, source.shape[3]), jnp.float32)
    row_views = phase_rows(source)
    for i in range(3):
        col_views = phase_cols(row_views[i])
        for j in range(3):
            window = col_views[j].astype(jnp.float32)
            summed = summed + window * weights[3 * i + j].astype(jnp.float32)
    return summed.astype(jnp.bfloat16)


def point_relu(spread, weights):
    shape_in = spread.shape
    mapped = jnp.dot(spread.reshape(-1, shape_in[3]), weights, preferred_element_type=jnp.float32)
    return jnp.maximum(mapped, 0.0).astype(jnp.bfloat16).reshape(shape_in[:3] + (weights.shape[1],))


def subsample(block_panels, block_lengths, conv_first, depth_a, point_a, depth_b, point_b):
    number = block_panels.shape[0]
    frames_in = block_panels.reshape(number, PANEL, MELS)
    inside = jnp.arange(PANEL)[None, :] < block_lengths[:, None]
    masked = jnp.where(inside[:, :, None], frames_in, jnp.zeros_like(frames_in))
    first = first_section(masked, conv_first)
    second = point_relu(depth_stride(first, depth_a), point_a)
    fourth = point_relu(depth_stride(second, depth_b), point_b)
    return fourth.reshape(number * fourth.shape[1], fourth.shape[2] * fourth.shape[3])


def depth_forward(gated, kernel, span):
    groups_in = gated.shape[0] // span
    half_width = kernel.shape[0] // 2
    shaped = jnp.pad(gated.reshape(groups_in, span, -1), ((0, 0), (half_width, half_width), (0, 0)))
    summed = jnp.zeros((groups_in, span, gated.shape[1]), jnp.float32)
    for k in range(kernel.shape[0]):
        summed = summed + shaped[:, k : k + span].astype(jnp.float32) * kernel[k].astype(
            jnp.float32
        )
    return summed.reshape(gated.shape[0], -1)


def depth_backward(upstream, kernel, span):
    groups_in = upstream.shape[0] // span
    half_width = kernel.shape[0] // 2
    shaped = jnp.pad(
        upstream.reshape(groups_in, span, -1), ((0, 0), (half_width, half_width), (0, 0))
    )
    summed = jnp.zeros((groups_in, span, upstream.shape[1]), jnp.float32)
    for k in range(kernel.shape[0]):
        offset = 2 * half_width - k
        summed = summed + shaped[:, offset : offset + span] * kernel[k].astype(jnp.float32)
    return summed.reshape(upstream.shape[0], -1)


def module_pass(
    features, keep, cotangent, norm_gain, up_weight, depth_kernel, conv_gain, down_weight, span
):
    width = features.shape[1]
    values = features.astype(jnp.float32)
    centred = values - jnp.mean(values, axis=1, keepdims=True)
    scale_one = lax.rsqrt(jnp.mean(centred * centred, axis=1, keepdims=True) + EPSILON)
    standard = centred * scale_one
    normed = (standard * norm_gain.astype(jnp.float32)).astype(jnp.bfloat16)
    projected = jnp.dot(normed, up_weight, preferred_element_type=jnp.float32)
    value_half = projected[:, :width]
    gate_half = jax.nn.sigmoid(projected[:, width:])
    row_keep = keep[:, None]
    gated = (row_keep * value_half * gate_half).astype(jnp.bfloat16)
    depthwise = depth_forward(gated, depth_kernel, span)
    centred_two = depthwise - jnp.mean(depthwise, axis=1, keepdims=True)
    scale_two = lax.rsqrt(jnp.mean(centred_two * centred_two, axis=1, keepdims=True) + EPSILON)
    standard_two = centred_two * scale_two
    active = standard_two * conv_gain.astype(jnp.float32)
    swish_gate = jax.nn.sigmoid(active)
    hidden = (active * swish_gate).astype(jnp.bfloat16)
    mixed = jnp.dot(hidden, down_weight, preferred_element_type=jnp.float32)
    layer_out = (row_keep * (values + mixed)).astype(jnp.bfloat16)
    back_out = jnp.where(row_keep > 0, cotangent, jnp.zeros_like(cotangent))
    back_hidden = lax.dot_general(
        back_out, down_weight, (((1,), (1,)), ((), ())), preferred_element_type=jnp.float32
    )
    back_active = back_hidden * (swish_gate + active * swish_gate * (1.0 - swish_gate))
    gain_back = back_active * conv_gain.astype(jnp.float32)
    back_depth = scale_two * (
        gain_back
        - jnp.mean(gain_back, axis=1, keepdims=True)
        - standard_two * jnp.mean(gain_back * standard_two, axis=1, keepdims=True)
    )
    back_gated = row_keep * depth_backward(back_depth, depth_kernel, span)
    back_proj = jnp.concatenate(
        [back_gated * gate_half, back_gated * value_half * gate_half * (1.0 - gate_half)], axis=1
    ).astype(jnp.bfloat16)
    back_normed = lax.dot_general(
        back_proj, up_weight, (((1,), (1,)), ((), ())), preferred_element_type=jnp.float32
    )
    gain_front = back_normed * norm_gain.astype(jnp.float32)
    back_input = scale_one * (
        gain_front
        - jnp.mean(gain_front, axis=1, keepdims=True)
        - standard * jnp.mean(gain_front * standard, axis=1, keepdims=True)
    )
    grad_input = (back_out.astype(jnp.float32) + back_input).astype(jnp.bfloat16)
    return (layer_out, grad_input, hidden, back_out)


def local(
    mel_panels,
    frames,
    target,
    conv_first,
    depth_a,
    point_a,
    depth_b,
    point_b,
    linear_weight,
    norm_gain,
    up_weight,
    depth_kernel,
    conv_gain,
    down_weight,
    cotangent,
):
    groups = lax.axis_size("dp")
    members = lax.axis_size("fsdp")
    span = PANEL // 8
    panel_count = cotangent.shape[0] // span
    destinations = jnp.arange(groups, dtype=jnp.int32)
    selected = (target[None, :] == destinations[:, None]) & (frames[None, :] > 0)
    outgoing = jnp.dot(
        selected.astype(jnp.bfloat16), mel_panels, preferred_element_type=jnp.float32
    ).astype(jnp.bfloat16)
    sent_frames = jnp.sum(jnp.where(selected, frames[None, :], 0), axis=1)
    incoming, got_frames = (
        lax.all_to_all(outgoing, "dp", split_axis=0, concat_axis=0, tiled=True),
        lax.all_to_all(sent_frames, "dp", split_axis=0, concat_axis=0, tiled=True),
    )
    present = got_frames > 0
    position = jnp.cumsum(present.astype(jnp.int32)) - 1
    places = jnp.arange(panel_count, dtype=jnp.int32)
    placing = (position[None, :] == places[:, None]) & present[None, :]
    panels = jnp.dot(
        placing.astype(jnp.bfloat16), incoming, preferred_element_type=jnp.float32
    ).astype(jnp.bfloat16)
    lengths = jnp.sum(jnp.where(placing, got_frames[None, :], 0), axis=1).astype(jnp.int32)
    first_full, depth_one, point_one, depth_two, point_two, gain_front, kernel_full, gain_back = (
        *sent_together((conv_first, depth_a, point_a, depth_b, point_b), "fsdp", 1, 0),
        lax.all_gather(norm_gain, "fsdp", axis=0, tiled=True),
        lax.all_gather(depth_kernel, "fsdp", axis=1, tiled=True),
        lax.all_gather(conv_gain, "fsdp", axis=0, tiled=True),
    )
    per_block = math.gcd(panel_count, 16)

    def sub_block(block_args):
        return subsample(
            block_args[0], block_args[1], first_full, depth_one, point_one, depth_two, point_two
        )

    flat_rows = lax.map(
        sub_block,
        (
            panels.reshape(panel_count // per_block, per_block, -1),
            lengths.reshape(panel_count // per_block, per_block),
        ),
    )
    flat_rows = flat_rows.reshape(panel_count * span, -1)
    features = jnp.dot(
        flat_rows,
        lax.all_gather(linear_weight, "fsdp", axis=1, tiled=True),
        preferred_element_type=jnp.float32,
    ).astype(jnp.bfloat16)
    keep = (jnp.arange(span)[None, :] < (lengths // 8)[:, None]).reshape(-1).astype(jnp.float32)
    up_full, down_full = gather_together((up_weight, down_weight), "fsdp", (1, 0))
    layer_out, grad_input, hidden, back_out = module_pass(
        features, keep, cotangent, gain_front, up_full, kernel_full, gain_back, down_full, span
    )
    local_rows = sent_and_summed(
        lax.dot_general(
            hidden, back_out, (((0,), (0,)), ((), ())), preferred_element_type=jnp.float32
        ).astype(jnp.bfloat16),
        "fsdp",
        0,
    )
    summed = lax.psum(local_rows, "dp")
    grad_down = summed / jnp.sqrt(jnp.float32(cotangent.shape[0] * groups * members))
    return (layer_out, grad_input, grad_down)


def solution(mesh):
    placed = (
        P(("dp", "fsdp"), None),
        P(("dp", "fsdp")),
        P(("dp", "fsdp")),
        P(None, "fsdp"),
        P(None, "fsdp"),
        P(None, "fsdp"),
        P(None, "fsdp"),
        P(None, "fsdp"),
        P(None, "fsdp"),
        P("fsdp"),
        P(None, "fsdp"),
        P(None, "fsdp"),
        P("fsdp"),
        P("fsdp", None),
        P(("dp", "fsdp"), None),
    )
    return jax.shard_map(
        local,
        mesh=mesh,
        in_specs=placed,
        out_specs=(P(("dp", "fsdp"), None), P(("dp", "fsdp"), None), P("fsdp", None)),
        check_vma=False,
    )
```

profile of v0, /device:TPU:0, one launch (start us, length us, event | category | flops | bytes accessed | tf_op | source)
XLA Modules:
  0.0 737.0 jit_solution(10071461535330743551)
XLA Ops:
  10.0 11.8 %all-to-all-start = ((s32[64,1,1]{2,1,0:T(1,128)}), s32[64,1,1]{2,1,0:T(1,128)}, u32[]{:S(2)}, u32[]{:S(2)}) async-start(s32[64,1,1]{2,1,0:T(1,128)} %copy.218), calls=%async_computation | async-start | bytes 65536 | tf_op jit(solution)/shard_map/all_to_all | solution.py:212
  24.1 10.4 %pad_maximum_fusion = bf16[1572864]{0:T(1024)(128)(2,1)} fusion(bf16[524288]{0:T(1024)(128)(2,1)S(1)} %bitcast.397, bf16[1048576]{0:T(1024)(128)(2,1)S(1)} %bitcast.392), kind=kLoop, calls=%fused_computation.103 | loop fusion | flops 6291456 | bytes 6291456 | tf_op jit(solution)/shard_map/concatenate | solution.py:26
  51.2 10.1 %all-to-all-start.1 = ((bf16[64,2,5120]{2,1,0:T(2,128)(2,1)}), bf16[64,2,5120]{2,1,0:T(2,128)(2,1)S(1)}, u32[]{:S(2)}, u32[]{:S(2)}) async-start(bf16[64,2,5120]{2,1,0:T(2,128)(2,1)} %reshape.638), calls=%async_computation.1 | async-start | bytes 2621440 | tf_op jit(solution)/shard_map/all_to_all | solution.py:211
  65.3 18.0 %all-to-all-done.1 = bf16[64,2,5120]{2,1,0:T(2,128)(2,1)S(1)} async-done(((bf16[64,2,5120]{2,1,0:T(2,128)(2,1)}), bf16[64,2,5120]{2,1,0:T(2,128)(2,1)S(1)}, u32[]{:S(2)}, u32[]{:S(2)}) %all-to-all-start.1) | async-done | bytes 1310752 | tf_op jit(solution)/shard_map/all_to_all | solution.py:211
  83.3 3.6 reshape.639
  86.9 3.5 convolution_convert_fusion.1
  90.4 445.1 %while.10 = (s32[]{:T(128)}, bf16[2,256,2560]{2,1,0:T(8,128)(2,1)}, s32[2,16]{1,0:T(2,128)S(1)}, bf16[2,16,10240]{2,1,0:T(8,128)(2,1)}, bf16[9,256]{1,0:T(8,128)...) while((s32[]{:T(128)}, bf16[2,256,2560]{2,1,0:T(8,128)(2,1)}, ...), condition=%wide.region_4.5_spmd, body=%wide.region_3.4_spmd.sunk | while | flops 1972519936 | bytes 356025408 | solution.py:235
  146.4 54.4 %maximum_convert_fusion.2 = bf16[16,32,2,40,256]{4,1,3,0,2:T(8,128)(2,1)} fusion(f32[256]{0:T(256)S(1)} %bitcast.422, f32[16,32,2,40]{1,3,0,2:T(8,128)S(1)} %copy.284, f32[256]{0:T(256)S(1)} %bitcast.423, f32[16,32,2,40]{1,3,0,2:T(8,128)} %copy.286, f32[256]{0:T(256)S(1)} %bitcast.424, f32[16,32,2,40]{1,3,0,2:T(8,128)S(1)} %copy.289, ...), kind=kLoop, calls=%fused_computation.clone.1 | loop fusion | flops 199229440 | bytes 22455296 | tf_op jit(solution)/shard_map/while/body/eval_jaxpr/convert_element_type | solution.py:74
  200.8 17.6 %slice_bitcast_fusion.22 = (bf16[16,32,40,256]{3,1,2,0:T(8,128)(2,1)}, bf16[16,32,1,40,256]{4,1,3,0,2:T(8,128)(2,1)S(1)}, bf16[16,32,1,40,256]{4,1,3,0,2:T(8,128)(2,1)}) fusion(bf16[16,32,2,40,256]{4,1,3,0,2:T(8,128)(2,1)} %maximum_convert_fusion.2), kind=kLoop, calls=%fused_computation.89.clone.1 | loop fusion | bytes 52428800 | tf_op jit(solution)/shard_map/while/body/eval_jaxpr/squeeze | solution.py:50
  218.4 8.7 %concatenate.77 = bf16[16,32,40,256]{3,1,2,0:T(8,128)(2,1)S(1)} pad(bf16[16,31,40,256]{3,1,2,0:T(8,128)(2,1)} %bitcast.367, bf16[]{:T(256)} %constant.45.clone.7..sunk), padding=0_0x1_0x0_0x0_0 | pad | bytes 20643842 | tf_op jit(solution)/shard_map/while/body/eval_jaxpr/concatenate | solution.py:51
  227.1 3.2 slice_bitcast_fusion.25
  230.3 5.2 slice.622
  235.5 5.6 slice_bitcast_fusion.23
  241.1 5.3 slice.620
  246.4 3.2 slice_bitcast_fusion.24
  249.6 5.3 slice.621
  254.9 14.6 %fusion.121 = bf16[16,32,20,256]{3,1,2,0:T(8,128)(2,1)} fusion(bf16[16,32,20,2,256]{4,1,3,2,0:T(8,128)(2,1)} %bitcast.366, bf16[16,32,20,2,256]{4,1,3,2,0:T(8,128)(2,1)S(1)} %bitcast.364, bf16[16,32,20,2,256]{4,1,3,2,0:T(8,128)(2,1)S(1)} %bitcast.362, f32[256]{0:T(256)S(1)} %bitcast.410, f32[256]{0:T(256)S(1)} %bitcast.409, f32[256]{0:T(256)S(1)} %bitcast.408, ...), kind=kLoop, calls=%fused_computation.6.clone.1 | loop fusion | flops 70778880 | bytes 51651584 | tf_op jit(solution)/shard_map/while/body/eval_jaxpr/convert_element_type | solution.py:87
  269.5 8.9 %copy.307 = bf16[16,32,20,256]{3,2,1,0:T(8,128)(2,1)} copy(bf16[16,32,20,256]{3,1,2,0:T(8,128)(2,1)} %fusion.121) | data formatting | bytes 10485760 | tf_op jit(solution)/shard_map/while/body/eval_jaxpr/convert_element_type | solution.py:87
  278.4 9.0 %reshape.645 = bf16[10240,256]{1,0:T(8,128)(2,1)} reshape(bf16[16,32,20,256]{3,2,1,0:T(8,128)(2,1)} %copy.307) | data formatting | bytes 10485760 | tf_op jit(solution)/shard_map/while/body/eval_jaxpr/reshape | solution.py:92
  287.4 6.3 fusion.122
  293.6 8.9 %reshape.646 = bf16[16,16,2,20,256]{4,3,2,1,0:T(8,128)(2,1)} reshape(bf16[10240,256]{1,0:T(8,128)(2,1)} %fusion.122) | data formatting | bytes 10485760 | tf_op jit(solution)/shard_map/while/body/eval_jaxpr/reshape;while/body/eval_jaxpr/reshape | solution.py:48
  302.5 3.5 slice_bitcast_fusion.26
  355.1 54.4 %maximum_convert_fusion.2 = bf16[16,32,2,40,256]{4,1,3,0,2:T(8,128)(2,1)} fusion(f32[256]{0:T(256)S(1)} %bitcast.422, f32[16,32,2,40]{1,3,0,2:T(8,128)S(1)} %copy.284, f32[256]{0:T(256)S(1)} %bitcast.423, f32[16,32,2,40]{1,3,0,2:T(8,128)} %copy.286, f32[256]{0:T(256)S(1)} %bitcast.424, f32[16,32,2,40]{1,3,0,2:T(8,128)S(1)} %copy.289, ...), kind=kLoop, calls=%fused_computation.clone.1 | loop fusion | flops 199229440 | bytes 22455296 | tf_op jit(solution)/shard_map/while/body/eval_jaxpr/convert_element_type | solution.py:74
  409.5 17.6 %slice_bitcast_fusion.22 = (bf16[16,32,40,256]{3,1,2,0:T(8,128)(2,1)}, bf16[16,32,1,40,256]{4,1,3,0,2:T(8,128)(2,1)S(1)}, bf16[16,32,1,40,256]{4,1,3,0,2:T(8,128)(2,1)}) fusion(bf16[16,32,2,40,256]{4,1,3,0,2:T(8,128)(2,1)} %maximum_convert_fusion.2), kind=kLoop, calls=%fused_computation.89.clone.1 | loop fusion | bytes 52428800 | tf_op jit(solution)/shard_map/while/body/eval_jaxpr/squeeze | solution.py:50
  427.1 8.7 %concatenate.77 = bf16[16,32,40,256]{3,1,2,0:T(8,128)(2,1)S(1)} pad(bf16[16,31,40,256]{3,1,2,0:T(8,128)(2,1)} %bitcast.367, bf16[]{:T(256)} %constant.45.clone.7..sunk), padding=0_0x1_0x0_0x0_0 | pad | bytes 20643842 | tf_op jit(solution)/shard_map/while/body/eval_jaxpr/concatenate | solution.py:51
  435.8 3.2 slice_bitcast_fusion.25
  439.0 5.2 slice.622
  444.2 5.6 slice_bitcast_fusion.23
  449.8 5.3 slice.620
  455.1 3.2 slice_bitcast_fusion.24
  458.2 5.3 slice.621
  463.5 14.6 %fusion.121 = bf16[16,32,20,256]{3,1,2,0:T(8,128)(2,1)} fusion(bf16[16,32,20,2,256]{4,1,3,2,0:T(8,128)(2,1)} %bitcast.366, bf16[16,32,20,2,256]{4,1,3,2,0:T(8,128)(2,1)S(1)} %bitcast.364, bf16[16,32,20,2,256]{4,1,3,2,0:T(8,128)(2,1)S(1)} %bitcast.362, f32[256]{0:T(256)S(1)} %bitcast.410, f32[256]{0:T(256)S(1)} %bitcast.409, f32[256]{0:T(256)S(1)} %bitcast.408, ...), kind=kLoop, calls=%fused_computation.6.clone.1 | loop fusion | flops 70778880 | bytes 51651584 | tf_op jit(solution)/shard_map/while/body/eval_jaxpr/convert_element_type | solution.py:87
  478.2 8.9 %copy.307 = bf16[16,32,20,256]{3,2,1,0:T(8,128)(2,1)} copy(bf16[16,32,20,256]{3,1,2,0:T(8,128)(2,1)} %fusion.121) | data formatting | bytes 10485760 | tf_op jit(solution)/shard_map/while/body/eval_jaxpr/convert_element_type | solution.py:87
  487.1 9.0 %reshape.645 = bf16[10240,256]{1,0:T(8,128)(2,1)} reshape(bf16[16,32,20,256]{3,2,1,0:T(8,128)(2,1)} %copy.307) | data formatting | bytes 10485760 | tf_op jit(solution)/shard_map/while/body/eval_jaxpr/reshape | solution.py:92
  496.0 6.3 fusion.122
  502.3 8.9 %reshape.646 = bf16[16,16,2,20,256]{4,3,2,1,0:T(8,128)(2,1)} reshape(bf16[10240,256]{1,0:T(8,128)(2,1)} %fusion.122) | data formatting | bytes 10485760 | tf_op jit(solution)/shard_map/while/body/eval_jaxpr/reshape;while/body/eval_jaxpr/reshape | solution.py:48
  511.2 3.5 slice_bitcast_fusion.26
  535.6 6.2 convert_reduce_fusion.1
  542.3 6.9 reshape.629
  554.8 3.3 copy.250
  558.1 6.2 copy.221
  564.3 4.6 fusion.63
  571.1 3.0 fusion.79
  574.6 5.0 reshape_reshape.3
  590.2 5.7 all_to_all.29
  598.9 5.5 multiply_reduce_fusion.2
  610.5 116.3 %all-reduce.16.cloned.1.call-done = f32[512,1024]{1,0:T(8,128)} async-done(((f32[512,1024]{1,0:T(8,128)}), f32[512,1024]{1,0:T(8,128)}) %all-reduce.16.cloned.1.call-update) | async-done | bytes 2097168 | tf_op jit(solution)/shard_map/psum | solution.py:260
  726.8 3.2 broadcast_multiply_fusion
  (289 shorter events, 151.4 us)
Async XLA Ops:
  7.2 32.2 %copy-start = (bf16[64,10240]{1,0:T(8,128)(2,1)S(1)}, bf16[64,10240]{1,0:T(8,128)(2,1)}, u32[]{:S(2)}) copy-start(bf16[64,10240]{1,0:T(8,128)(2,1)} %param.17) | copy-start | bytes 3932164
  7.2 15.4 %copy-start.10 = (bf16[1024,1024]{1,0:T(8,128)(2,1)S(1)}, bf16[1024,1024]{1,0:T(8,128)(2,1)}, u32[]{:S(2)}) copy-start(bf16[1024,1024]{1,0:T(8,128)(2,1)} %param.27) | copy-start | bytes 6291460
  10.0 41.2 %all-to-all-start = ((s32[64,1,1]{2,1,0:T(1,128)}), s32[64,1,1]{2,1,0:T(1,128)}, u32[]{:S(2)}, u32[]{:S(2)}) async-start(s32[64,1,1]{2,1,0:T(1,128)} %copy.218), calls=%async_computation | async-start | bytes 65536 | tf_op jit(solution)/shard_map/all_to_all | solution.py:212
  21.8 513.8 %all-gather.6.cloned.1.call-start = ((), (), s32[]{:S(2)}) async-start(), calls=%async_computation.3 | async-start | bytes 7864320 | tf_op jit(solution)/shard_map/all_gather | solution.py:245
  22.6 519.7 %all-gather.8.cloned.1.call-start = ((), (), s32[]{:S(2)}) async-start(), calls=%async_computation.5 | async-start | bytes 9437184 | tf_op jit(solution)/shard_map/all_gather | solution.py:27
  34.5 4.8 copy-start.38
  34.5 4.8 copy-start.40
  35.4 4.4 copy-start.41
  35.4 6.3 copy-start.33
  35.4 8.8 %copy-start.42 = (bf16[512]{0:T(512)(128)(2,1)S(1)}, bf16[512]{0:T(512)(128)(2,1)}, u32[]{:S(2)}) copy-start(bf16[512]{0:T(512)(128)(2,1)} %param.29) | copy-start | bytes 3076
  51.2 32.1 %all-to-all-start.1 = ((bf16[64,2,5120]{2,1,0:T(2,128)(2,1)}), bf16[64,2,5120]{2,1,0:T(2,128)(2,1)S(1)}, u32[]{:S(2)}, u32[]{:S(2)}) async-start(bf16[64,2,5120]{2,1,0:T(2,128)(2,1)} %reshape.638), calls=%async_computation.1 | async-start | bytes 2621440 | tf_op jit(solution)/shard_map/all_to_all | solution.py:211
  61.3 665.5 %all-reduce.16.cloned.1.call-start = ((), (), s32[]{:S(2)}) async-start(), calls=%async_computation.4 | async-start | bytes 4194304 | tf_op jit(solution)/shard_map/psum | solution.py:260
  64.8 25.7 %copy-start.29 = (f32[512]{0:T(512)}, f32[512]{0:T(512)S(1)}, u32[]{:S(2)}) copy-start(f32[512]{0:T(512)S(1)} %reshape.619) | copy-start | bytes 6148
  111.0 5.2 copy-start.43
  111.1 143.8 %copy-start.16 = (bf16[9,256]{1,0:T(8,128)(2,1)}, bf16[9,256]{1,0:T(8,128)(2,1)S(1)}, u32[]{:S(2)}) copy-start(bf16[9,256]{1,0:T(8,128)(2,1)S(1)} %get-tuple-element.321) | copy-start | bytes 13828 | tf_op jit(solution)/shard_map/while
  310.5 1.3 slice-start
  310.5 1.6 slice-start.1
  317.0 2.7 copy-start.17
  317.0 2.7 copy-start.44
  319.7 5.2 copy-start.43
  319.7 143.8 %copy-start.16 = (bf16[9,256]{1,0:T(8,128)(2,1)}, bf16[9,256]{1,0:T(8,128)(2,1)S(1)}, u32[]{:S(2)}) copy-start(bf16[9,256]{1,0:T(8,128)(2,1)S(1)} %get-tuple-element.321) | copy-start | bytes 13828 | tf_op jit(solution)/shard_map/while
  519.2 1.3 slice-start
  519.2 1.6 slice-start.1
  525.7 2.7 copy-start.17
  525.7 2.7 copy-start.44
  541.8 22.5 %copy-start.7 = (bf16[512,1024]{1,0:T(8,128)(2,1)}, bf16[512,1024]{1,0:T(8,128)(2,1)S(1)}, u32[]{:S(2)}) copy-start(bf16[512,1024]{1,0:T(8,128)(2,1)S(1)} %get-tuple-element.146) | copy-start | bytes 3145732
  549.3 2.8 copy-start.4
  552.0 2.8 slice-start.2
  558.1 6.2 copy-start.32
  564.3 4.6 copy-start.30
  569.0 2.0 copy-start.5
  569.0 2.0 copy-start.20
  569.0 2.0 copy-start.21
  569.0 2.0 copy-start.22
  569.0 2.0 copy-start.23
  569.0 2.0 copy-start.24
  569.0 2.0 copy-start.25
  569.0 2.0 copy-start.26
  569.1 2.0 copy-start.27
  569.1 2.0 copy-start.28
  579.5 1.6 copy-start.11
  579.5 1.9 copy-start.14
  579.5 1.9 copy-start.31
  579.6 1.9 copy-start.37
  584.5 2.3 copy-start.6
  598.9 5.5 copy-start.15
  606.3 2.0 copy-start.12
  608.2 121.8 %copy-start.1 = (bf16[64,10240]{1,0:T(8,128)(2,1)S(1)}, bf16[64,10240]{1,0:T(8,128)(2,1)}, u32[]{:S(2)}) copy-start(bf16[64,10240]{1,0:T(8,128)(2,1)} %param.17) | copy-start | bytes 3932164
  (13 other events, 12.9 us)
Sparse Core Ops, SparseCore 0:
  24.3 19.1 all-gather.5
  45.1 20.8 all-gather.7
  597.8 128.9 all-reduce.15
where the time goes:
time: 749 us; the launch traced here: 737 us
  local copies, waits for them, and re-layouts  292 us (39%)
  other arithmetic  190 us (25%)
  waiting for transfers between devices  135 us (18%)
  matrix products  41.8 us (6%)
  loops' own time  28.4 us (4%)
  starting transfers between devices  22 us (3%)
  between operations  14.7 us (2%)
  blocking collectives  13.3 us (2%)
    psum x1, waiting for transfers between devices, local(): summed = lax.psum(local_rows, 'dp')  116 us
    convert_element_type x2, other arithmetic, first_section(): return jnp.maximum(summed, 0.0).astype(jnp.bfloat16)  109 us
    mul x36, local copies, waits for them, and re-layouts, first_section(): window[:, :, :, None] * weights[3 * i + j].astype(jnp.float32)  46.2 us
    squeeze x4, local copies, waits for them, and re-layouts, phase_rows(): odd = split[:, :, 1]  42.2 us
    slice x16, local copies, waits for them, and re-layouts, phase_cols(): odd[:, :, :-1]  34.4 us
    convert_element_type x4, other arithmetic, depth_stride(): return summed.astype(jnp.bfloat16)  33.9 us
    another operation x1, loops' own time, local(): lax.map(sub_block, (panels.reshape(panel_count // per_block, per_block, -...  28.4 us
    squeeze x12, local copies, waits for them, and re-layouts, phase_cols(): odd = split[:, :, :, 1]  24.9 us
  transfers between devices with their start and end apart: 5, of which 2 were waited for; matrix products, arithmetic and copies ran while one was open for 62% of the time, Pallas kernels for 0%

commit v1 on v0

--- a/solution.py
+++ b/solution.py
@@ -257,7 +257,7 @@
         "fsdp",
         0,
     )
-    summed = lax.psum(local_rows, "dp")
+    summed = jnp.sum(lax.all_gather(local_rows, "dp"), 0)
     grad_down = summed / jnp.sqrt(jnp.float32(cotangent.shape[0] * groups * members))
     return (layer_out, grad_input, grad_down)
 

time: 749 us -> 1150 us (1.54)
  waiting for transfers between devices: 135 us -> 513 us
  other arithmetic: 190 us -> 226 us
    all_gather x0 -> x1, waiting for transfers between devices: none -> 493 us  [local(): summed = jnp.sum(lax.all_gather(local_rows, 'dp'), 0)]
    psum x1 -> x0, waiting for transfers between devices: 116 us -> none  [local(): summed = lax.psum(local_rows, 'dp')]
    reduce_sum x0 -> x1, other arithmetic: none -> 40.6 us  [local(): summed = jnp.sum(lax.all_gather(local_rows, 'dp'), 0)]
  transfers between devices with their start and end apart: 5 -> 5, of which waited for: 2 -> 2; matrix products, arithmetic and copies ran while one was open for 62% -> 39% of each run, Pallas kernels for 0% -> 0%
where the time goes in v1:
time: 1150 us; the launch traced here: 1140 us
  waiting for transfers between devices  513 us (45%)
  local copies, waits for them, and re-layouts  285 us (25%)
  other arithmetic  226 us (20%)
  matrix products  38.6 us (3%)
  loops' own time  30 us (3%)
  starting transfers between devices  22 us (2%)
  between operations  14.5 us (1%)
  blocking collectives  12.9 us (1%)
    all_gather x1, waiting for transfers between devices, local(): summed = jnp.sum(lax.all_gather(local_rows, 'dp'), 0)  493 us
    convert_element_type x2, other arithmetic, first_section(): return jnp.maximum(summed, 0.0).astype(jnp.bfloat16)  109 us
    mul x36, local copies, waits for them, and re-layouts, first_section(): window[:, :, :, None] * weights[3 * i + j].astype(jnp.float32)  46 us
    reduce_sum x1, other arithmetic, local(): summed = jnp.sum(lax.all_gather(local_rows, 'dp'), 0)  40.6 us
    slice x16, local copies, waits for them, and re-layouts, phase_cols(): odd[:, :, :-1]  37.6 us
    squeeze x4, local copies, waits for them, and re-layouts, phase_rows(): odd = split[:, :, 1]  35.2 us
    convert_element_type x4, other arithmetic, depth_stride(): return summed.astype(jnp.bfloat16)  33.9 us
    another operation x1, loops' own time, local(): lax.map(sub_block, (panels.reshape(panel_count // per_block, per_block, -...  30 us
  transfers between devices with their start and end apart: 5, of which 2 were waited for; matrix products, arithmetic and copies ran while one was open for 39% of the time, Pallas kernels for 0%

profile of v1, /device:TPU:0, one launch (start us, length us, event | category | flops | bytes accessed | tf_op | source)
XLA Modules:
  0.0 1141.9 jit_solution(11466798984186020646)
XLA Ops:
  8.8 11.5 %all-to-all-start = ((s32[64,1,1]{2,1,0:T(1,128)}), s32[64,1,1]{2,1,0:T(1,128)S(1)}, u32[]{:S(2)}, u32[]{:S(2)}) async-start(s32[64,1,1]{2,1,0:T(1,128)} %copy.218), calls=%async_computation | async-start | bytes 65536 | tf_op jit(solution)/shard_map/all_to_all | solution.py:212
  22.7 10.4 pad_maximum_fusion
  49.5 10.3 all-to-all-start.1
  62.3 19.6 %all-to-all-done.1 = bf16[64,2,5120]{2,1,0:T(2,128)(2,1)S(1)} async-done(((bf16[64,2,5120]{2,1,0:T(2,128)(2,1)}), bf16[64,2,5120]{2,1,0:T(2,128)(2,1)S(1)}, u32[]{:S(2)}, u32[]{:S(2)}) %all-to-all-start.1) | async-done | bytes 1310752 | tf_op jit(solution)/shard_map/all_to_all | solution.py:211
  81.9 3.5 reshape.640
  85.4 3.5 convolution_convert_fusion.1
  88.9 434.0 %while.10 = (s32[]{:T(128)}, bf16[2,256,2560]{2,1,0:T(8,128)(2,1)}, s32[2,16]{1,0:T(2,128)S(1)}, bf16[2,16,10240]{2,1,0:T(8,128)(2,1)}, bf16[9,256]{1,0:T(8,128)...) while((s32[]{:T(128)}, bf16[2,256,2560]{2,1,0:T(8,128)(2,1)}, ...), condition=%wide.region_4.5_spmd, body=%wide.region_3.4_spmd.sunk | while | flops 1972519936 | bytes 399062016 | solution.py:235
  142.7 54.4 %maximum_convert_fusion.2 = bf16[16,32,2,40,256]{4,1,3,0,2:T(8,128)(2,1)} fusion(f32[256]{0:T(256)S(1)} %bitcast.423, f32[16,32,2,40]{1,3,0,2:T(8,128)S(1)} %copy.284, f32[256]{0:T(256)S(1)} %bitcast.424, f32[16,32,2,40]{1,3,0,2:T(8,128)} %copy.286, f32[256]{0:T(256)S(1)} %bitcast.425, f32[16,32,2,40]{1,3,0,2:T(8,128)S(1)} %copy.289, ...), kind=kLoop, calls=%fused_computation.clone.1 | loop fusion | flops 199229440 | bytes 22455296 | tf_op jit(solution)/shard_map/while/body/eval_jaxpr/convert_element_type | solution.py:74
  197.0 14.2 %slice_bitcast_fusion.22 = (bf16[16,32,40,256]{3,1,2,0:T(8,128)(2,1)}, bf16[16,32,1,40,256]{4,1,3,0,2:T(8,128)(2,1)S(1)}, bf16[16,32,1,40,256]{4,1,3,0,2:T(8,128)(2,1)S(1)}) fusion(bf16[16,32,2,40,256]{4,1,3,0,2:T(8,128)(2,1)} %maximum_convert_fusion.2), kind=kLoop, calls=%fused_computation.89.clone.1 | loop fusion | bytes 52428800 | tf_op jit(solution)/shard_map/while/body/eval_jaxpr/squeeze | solution.py:50
  211.2 3.5 slice_bitcast_fusion.24
  214.7 6.9 slice.621
  221.6 3.1 slice_bitcast_fusion.23
  224.7 5.3 slice.620
  230.0 8.7 concatenate.77
  238.8 3.1 slice_bitcast_fusion.25
  241.9 5.3 slice.622
  247.2 14.6 %fusion.121 = bf16[16,32,20,256]{3,1,2,0:T(8,128)(2,1)} fusion(bf16[16,32,20,2,256]{4,1,3,2,0:T(8,128)(2,1)} %bitcast.367, bf16[16,32,20,2,256]{4,1,3,2,0:T(8,128)(2,1)S(1)} %bitcast.365, bf16[16,32,20,2,256]{4,1,3,2,0:T(8,128)(2,1)S(1)} %bitcast.363, f32[256]{0:T(256)S(1)} %bitcast.411, f32[256]{0:T(256)S(1)} %bitcast.410, f32[256]{0:T(256)S(1)} %bitcast.409, ...), kind=kLoop, calls=%fused_computation.6.clone.1 | loop fusion | flops 70778880 | bytes 51651584 | tf_op jit(solution)/shard_map/while/body/eval_jaxpr/convert_element_type | solution.py:87
  261.8 8.9 copy.307
  270.7 9.0 reshape.646
  279.7 6.3 fusion.122
  286.0 8.9 reshape.647
  294.9 3.4 slice_bitcast_fusion.26
  345.1 54.4 %maximum_convert_fusion.2 = bf16[16,32,2,40,256]{4,1,3,0,2:T(8,128)(2,1)} fusion(f32[256]{0:T(256)S(1)} %bitcast.423, f32[16,32,2,40]{1,3,0,2:T(8,128)S(1)} %copy.284, f32[256]{0:T(256)S(1)} %bitcast.424, f32[16,32,2,40]{1,3,0,2:T(8,128)} %copy.286, f32[256]{0:T(256)S(1)} %bitcast.425, f32[16,32,2,40]{1,3,0,2:T(8,128)S(1)} %copy.289, ...), kind=kLoop, calls=%fused_computation.clone.1 | loop fusion | flops 199229440 | bytes 22455296 | tf_op jit(solution)/shard_map/while/body/eval_jaxpr/convert_element_type | solution.py:74
  399.5 14.2 %slice_bitcast_fusion.22 = (bf16[16,32,40,256]{3,1,2,0:T(8,128)(2,1)}, bf16[16,32,1,40,256]{4,1,3,0,2:T(8,128)(2,1)S(1)}, bf16[16,32,1,40,256]{4,1,3,0,2:T(8,128)(2,1)S(1)}) fusion(bf16[16,32,2,40,256]{4,1,3,0,2:T(8,128)(2,1)} %maximum_convert_fusion.2), kind=kLoop, calls=%fused_computation.89.clone.1 | loop fusion | bytes 52428800 | tf_op jit(solution)/shard_map/while/body/eval_jaxpr/squeeze | solution.py:50
  413.7 3.5 slice_bitcast_fusion.24
  417.2 6.9 slice.621
  424.1 3.1 slice_bitcast_fusion.23
  427.2 5.3 slice.620
  432.5 8.7 concatenate.77
  441.2 3.1 slice_bitcast_fusion.25
  444.4 5.3 slice.622
  449.6 14.6 %fusion.121 = bf16[16,32,20,256]{3,1,2,0:T(8,128)(2,1)} fusion(bf16[16,32,20,2,256]{4,1,3,2,0:T(8,128)(2,1)} %bitcast.367, bf16[16,32,20,2,256]{4,1,3,2,0:T(8,128)(2,1)S(1)} %bitcast.365, bf16[16,32,20,2,256]{4,1,3,2,0:T(8,128)(2,1)S(1)} %bitcast.363, f32[256]{0:T(256)S(1)} %bitcast.411, f32[256]{0:T(256)S(1)} %bitcast.410, f32[256]{0:T(256)S(1)} %bitcast.409, ...), kind=kLoop, calls=%fused_computation.6.clone.1 | loop fusion | flops 70778880 | bytes 51651584 | tf_op jit(solution)/shard_map/while/body/eval_jaxpr/convert_element_type | solution.py:87
  464.3 8.9 copy.307
  473.2 9.0 reshape.646
  482.2 6.3 fusion.122
  488.5 8.9 reshape.647
  497.4 3.4 slice_bitcast_fusion.26
  522.9 6.2 convert_reduce_fusion.1
  529.7 7.0 reshape.629
  536.6 7.9 slice.352
  544.5 3.3 reshape_reshape.3
  547.8 5.5 copy.250
  553.3 6.2 copy.221
  559.5 4.6 fusion.63
  571.6 4.0 fusion.78
  576.9 5.4 all_to_all.29
  600.1 492.9 %all-gather.12.cloned.1.call-done = f32[32768,1024]{1,0:T(8,128)} async-done(((f32[512,1024]{1,0:T(8,128)}), f32[32768,1024]{1,0:T(8,128)}) %all-gather.12.cloned.1.call-update) | async-done | bytes 134217744 | tf_op jit(solution)/shard_map/all_gather | solution.py:260
  1093.1 40.6 %reduce_sum.119 = f32[512,1024]{1,0:T(8,128)S(1)} reduce(f32[64,512,1024]{2,1,0:T(8,128)} %bitcast.87, f32[]{:T(128)} %constant.69.clone.1), dimensions={0}, to_apply=%region_14.15 | reduce | flops 33030144 | bytes 136314880 | tf_op jit(solution)/shard_map/reduce_sum | solution.py:260
  (340 shorter events, 143.7 us)
Async XLA Ops:
  7.2 37.3 %copy-start = (bf16[64,10240]{1,0:T(8,128)(2,1)S(1)}, bf16[64,10240]{1,0:T(8,128)(2,1)}, u32[]{:S(2)}) copy-start(bf16[64,10240]{1,0:T(8,128)(2,1)} %param.17) | copy-start | bytes 3932164
  7.2 14.8 %copy-start.12 = (bf16[1024,1024]{1,0:T(8,128)(2,1)S(1)}, bf16[1024,1024]{1,0:T(8,128)(2,1)}, u32[]{:S(2)}) copy-start(bf16[1024,1024]{1,0:T(8,128)(2,1)} %param.27) | copy-start | bytes 6291460
  7.2 515.7 %all-gather.8.cloned.1.call-start = ((), (), s32[]{:S(2)}) async-start(), calls=%async_computation.3 | async-start | bytes 7864320 | tf_op jit(solution)/shard_map/all_gather | solution.py:245
  8.8 40.7 %all-to-all-start = ((s32[64,1,1]{2,1,0:T(1,128)}), s32[64,1,1]{2,1,0:T(1,128)S(1)}, u32[]{:S(2)}, u32[]{:S(2)}) async-start(s32[64,1,1]{2,1,0:T(1,128)} %copy.218), calls=%async_computation | async-start | bytes 65536 | tf_op jit(solution)/shard_map/all_to_all | solution.py:212
  20.3 509.3 %all-gather.10.cloned.1.call-start = ((), (), s32[]{:S(2)}) async-start(), calls=%async_computation.4 | async-start | bytes 9437184 | tf_op jit(solution)/shard_map/all_gather | solution.py:27
  33.1 4.7 copy-start.51
  33.1 7.1 copy-start.52
  33.1 8.9 copy-start.45
  49.5 32.3 %all-to-all-start.1 = ((bf16[64,2,5120]{2,1,0:T(2,128)(2,1)}), bf16[64,2,5120]{2,1,0:T(2,128)(2,1)S(1)}, u32[]{:S(2)}, u32[]{:S(2)}) async-start(bf16[64,2,5120]{2,1,0:T(2,128)(2,1)} %reshape.639), calls=%async_computation.1 | async-start | bytes 2621440 | tf_op jit(solution)/shard_map/all_to_all | solution.py:211
  59.9 1033.2 %all-gather.12.cloned.1.call-start = ((), (), s32[]{:S(2)}) async-start(), calls=%async_computation.5 | async-start | bytes 136314880 | tf_op jit(solution)/shard_map/all_gather | solution.py:260
  61.8 27.1 %copy-start.41 = (f32[512]{0:T(512)}, f32[512]{0:T(512)S(1)}, u32[]{:S(2)}) copy-start(f32[512]{0:T(512)S(1)} %reshape.619) | copy-start | bytes 6148
  109.6 5.6 copy-start.17
  134.2 8.5 copy-start.28
  134.2 8.5 copy-start.29
  211.2 10.4 copy-start.2
  270.7 9.0 copy-start.7
  309.4 2.7 copy-start.18
  309.4 2.7 copy-start.55
  312.1 5.6 copy-start.17
  336.6 8.5 copy-start.28
  336.6 8.5 copy-start.29
  413.7 10.4 copy-start.2
  473.2 9.0 copy-start.7
  505.7 1.6 slice-start.1
  511.8 2.8 copy-start.18
  511.8 2.7 copy-start.55
  529.2 30.3 %copy-start.10 = (bf16[512,1024]{1,0:T(8,128)(2,1)}, bf16[512,1024]{1,0:T(8,128)(2,1)S(1)}, u32[]{:S(2)}) copy-start(bf16[512,1024]{1,0:T(8,128)(2,1)S(1)} %get-tuple-element.146) | copy-start | bytes 3145732
  536.6 7.9 slice-start.2
  553.3 6.2 copy-start.43
  559.5 4.6 copy-start.42
  564.1 2.0 copy-start.5
  564.1 2.0 copy-start.32
  564.2 2.0 copy-start.33
  564.2 2.0 copy-start.34
  564.2 2.0 copy-start.35
  564.2 2.0 copy-start.36
  564.2 2.0 copy-start.37
  564.2 2.0 copy-start.38
  564.2 2.0 copy-start.39
  564.2 2.0 copy-start.40
  569.7 1.9 copy-start.15
  569.7 1.9 copy-start.44
  569.7 1.8 copy-start.49
  586.3 2.3 copy-start.6
  588.6 2.7 copy-start.9
  588.6 3.2 copy-start.11
  591.8 2.6 copy-start.16
  1093.1 42.1 %copy-start.1 = (bf16[64,10240]{1,0:T(8,128)(2,1)S(1)}, bf16[64,10240]{1,0:T(8,128)(2,1)}, u32[]{:S(2)}) copy-start(bf16[64,10240]{1,0:T(8,128)(2,1)} %param.17) | copy-start | bytes 3932164
  (38 other events, 49.1 us)
Sparse Core Ops, SparseCore 0:
  9.7 20.3 all-gather.7
  33.2 20.7 all-gather.9
  584.3 508.7 all-gather.11
